TPU v7x, 512 devices: a whole 4x4x16 slice. The times are simulated.
512 devices in a mesh: seq: 128 (over z, x, core), dp: 4 (over y).
Axes of the slice: x: 4, y: 4, z: 16, core: 2. Of those that a mesh axis runs over, the one named last changes fastest.
Arguments:
- queries: bfloat16 [8192, 512], P(('dp', 'seq')), parts along dimension 0, may hold values from -6 to 6
- keys: bfloat16 [8192, 512], P(('dp', 'seq')), parts along dimension 0, may hold values from -6 to 6
- values: bfloat16 [8192, 512], P(('dp', 'seq')), parts along dimension 0, may hold values from -6 to 6
- residual: bfloat16 [8192, 1024], P(('dp', 'seq')), parts along dimension 0, may hold values from -16 to 16
- lengths: int32 [4], P('dp'), parts along dimension 0, may hold values from 1024 to 2048
- out_proj: bfloat16 [512, 1024], replicated, may hold values from -0.75 to 0.75
- ln_gain: float32 [1024], replicated, may hold values from 0.1 to 1.9
- ln_bias: float32 [1024], replicated, may hold values from -3 to 3
- conv_in: bfloat16 [1024, 1024], replicated, may hold values from -0.1875 to 0.1875
- taps: float32 [31, 512], replicated, may hold values from -1 to 1
- bn_scale: float32 [512], replicated, may hold values from 0.5 to 2
- bn_shift: float32 [512], replicated, may hold values from -3 to 3
- conv_out: bfloat16 [512, 1024], replicated, may hold values from -0.25 to 0.25
Outputs:
- block_out: bfloat16 [8192, 1024], P(('dp', 'seq')), parts along dimension 0
There are 4 independent parts, one for each index of `dp`. A program takes and returns all parts, laid end to end along the dimension named above; an argument that names none is the same for every part. Nothing has to cross between parts.
All inputs are finite; a program needn't handle non-finite values.
Results may differ from a plain program's by a relative error of at most 0.0075.
Values may be sent and summed in bfloat16 or wider, within the bound.
A program may use at most 64 MiB of HBM per device.

v0:
```python
import math

import jax
import jax.numpy as jnp
from jax import lax
from jax.sharding import PartitionSpec as P

HEAD_DIM = 64


def extended(block, sides, width):
    for axis, dim in sides:
        count = lax.axis_size(axis)
        forward = [(i, i + 1) for i in range(count - 1)]
        backward = [(target, source) for source, target in forward]
        low = lax.ppermute(
            lax.slice_in_dim(block, block.shape[dim] - width, None, axis=dim), axis, forward
        )
        high = lax.ppermute(lax.slice_in_dim(block, 0, width, axis=dim), axis, backward)
        block = jnp.concatenate([low, block, high], axis=dim)
    return block


def norm_lift(rows, row_frames, limit, ln_gain, ln_bias, conv_in):
    average = jnp.mean(rows, axis=-1, keepdims=True)
    centred = rows - average
    variance = jnp.mean(centred * centred, axis=-1, keepdims=True)
    normed = (centred * lax.rsqrt(variance + 1e-05) * ln_gain + ln_bias).astype(jnp.bfloat16)
    lifted = jnp.dot(normed, conv_in, preferred_element_type=jnp.float32)
    channels = conv_in.shape[1] // 2
    inside = ((row_frames >= 0) & (row_frames < limit)).astype(jnp.float32)
    return (inside[:, None] * lifted[:, :channels] * jax.nn.sigmoid(lifted[:, channels:])).astype(
        jnp.bfloat16
    )


def attend(carried, query_rows, key_block, value_block, key_frames, limit):
    running, totals, weighted = carried
    factor = 1.0 / math.sqrt(query_rows.shape[2])
    scores = (
        jnp.einsum("qhd,khd->hqk", query_rows, key_block, preferred_element_type=jnp.float32)
        * factor
    )
    scores = jnp.where((key_frames < limit)[None, None, :], scores, -1e30)
    highest = jnp.maximum(running, jnp.max(scores, axis=-1))
    rescale = jnp.exp(running - highest)
    powered = jnp.exp(scores - highest[:, :, None])
    totals = totals * rescale + jnp.sum(powered, axis=-1)
    weighted = weighted * jnp.transpose(rescale)[:, :, None] + jnp.einsum(
        "hqk,khd->qhd",
        powered.astype(jnp.bfloat16),
        value_block,
        preferred_element_type=jnp.float32,
    )
    return (highest, totals, weighted)


def split_pair(packed, columns, heads_here):
    row_count = packed.shape[0]
    key_part = packed[:, 0, :columns].reshape(row_count, heads_here, columns // heads_here)
    value_part = packed[:, 0, columns:].reshape(row_count, heads_here, columns // heads_here)
    return (key_part, value_part)


def on_device(
    queries,
    keys,
    values,
    residual,
    lengths,
    out_proj,
    ln_gain,
    ln_bias,
    conv_in,
    taps,
    bn_scale,
    bn_shift,
    conv_out,
):
    frames_here = residual.shape[0]
    width_att = queries.shape[1]
    devices = lax.axis_size("seq")
    position = lax.axis_index("seq")
    heads_all = width_att // HEAD_DIM
    groups = min(devices, heads_all)
    copies = devices // groups
    heads_here = heads_all // groups
    columns = heads_here * HEAD_DIM
    sub_rows = frames_here // copies
    query_count = devices * sub_rows
    limit = lengths[0]
    local_frames = position * frames_here + jnp.arange(frames_here, dtype=jnp.int32)
    valid_local = (local_frames < limit).astype(jnp.float32)
    query_rows = lax.all_to_all(
        queries.reshape(sub_rows, devices, columns), "seq", split_axis=1, concat_axis=0, tiled=True
    )
    carried = (
        jnp.full((heads_here, query_count), -1e30, jnp.float32),
        jnp.zeros((heads_here, query_count), jnp.float32),
        jnp.zeros((query_count, heads_here, HEAD_DIM), jnp.float32),
    )
    paired = jnp.concatenate(
        [
            keys.reshape(frames_here, 1, groups, columns),
            values.reshape(frames_here, 1, groups, columns),
        ],
        axis=3,
    )
    paired = jnp.broadcast_to(paired, (frames_here, copies, groups, 2 * columns)).reshape(
        frames_here, devices, 2 * columns
    )
    all_pairs = lax.all_to_all(paired, "seq", split_axis=1, concat_axis=0, tiled=True)
    block_size = groups * frames_here
    block_count = (limit + block_size - 1) // block_size

    def visit(number, looped):
        start = number * block_size
        current = lax.dynamic_slice_in_dim(all_pairs, start, block_size, 0)
        key_block, value_block = split_pair(current, columns, heads_here)
        key_frames = start + jnp.arange(block_size, dtype=jnp.int32)
        return attend(looped, query_rows, key_block, value_block, key_frames, limit)

    carried = lax.fori_loop(0, block_count, visit, carried)
    running, totals, weighted = carried
    context = (weighted / jnp.transpose(totals)[:, :, None]).astype(jnp.bfloat16)
    returned = lax.all_to_all(
        context.reshape(devices, sub_rows, 1, columns),
        "seq",
        split_axis=0,
        concat_axis=2,
        tiled=True,
    )
    context_here = returned.reshape(frames_here, width_att)
    mixed = residual.astype(jnp.float32) + valid_local[:, None] * jnp.dot(
        context_here, out_proj, preferred_element_type=jnp.float32
    )
    margin = taps.shape[0] // 2
    gated = norm_lift(mixed, local_frames, limit, ln_gain, ln_bias, conv_in)
    widened = extended(gated, (("seq", 0),), margin)
    widened = widened.astype(jnp.float32)
    filtered = taps[0] * widened[0:frames_here]
    for offset in range(1, taps.shape[0]):
        filtered = filtered + taps[offset] * widened[offset : offset + frames_here]
    shifted = filtered * bn_scale + bn_shift
    activated = (shifted * jax.nn.sigmoid(shifted)).astype(jnp.bfloat16)
    return (mixed + jnp.dot(activated, conv_out, preferred_element_type=jnp.float32)).astype(
        jnp.bfloat16
    )


def solution(mesh):
    placed = (
        P(("dp", "seq"), None),
        P(("dp", "seq"), None),
        P(("dp", "seq"), None),
        P(("dp", "seq"), None),
        P("dp"),
        P(),
        P(),
        P(),
        P(),
        P(),
        P(),
        P(),
        P(),
    )
    return jax.shard_map(
        on_device, mesh=mesh, in_specs=placed, out_specs=P(("dp", "seq"), None), check_vma=False
    )
```

profile of v0, /device:TPU:31, one launch (start us, length us, event | category | flops | bytes accessed | tf_op | source)
XLA Modules:
  0.0 132.5 jit_solution(11860965346838346635)
XLA Ops:
  0.0 1.6 %reshape.94 = bf16[1,128,64]{2,0,1:T(2,128)(2,1)} reshape(bf16[16,512]{1,0:T(8,128)(2,1)} %param.15) | data formatting | bytes 32768 | tf_op jit(solution)/shard_map/reshape | solution.py:95
  1.6 19.7 %all-to-all-start.1 = ((bf16[1,128,64]{2,0,1:T(2,128)(2,1)}), bf16[1,128,64]{2,0,1:T(2,128)(2,1)S(1)}, u32[]{:S(2)}, u32[]{:S(2)}) async-start(bf16[1,128,64]{2,0,1:T(2,128)(2,1)} %reshape.94), calls=%async_computation.1 | async-start | bytes 131072 | tf_op jit(solution)/shard_map/all_to_all | solution.py:94
  21.3 0.8 reshape.88
  22.1 0.8 reshape.89
  23.0 11.7 %all-to-all-done.1 = bf16[1,128,64]{2,0,1:T(2,128)(2,1)S(1)} async-done(((bf16[1,128,64]{2,0,1:T(2,128)(2,1)}), bf16[1,128,64]{2,0,1:T(2,128)(2,1)S(1)}, u32[]{:S(2)}, u32[]{:S(2)}) %all-to-all-start.1) | async-done | bytes 16416 | tf_op jit(solution)/shard_map/all_to_all | solution.py:94
  34.7 0.9 broadcast_in_dim.42
  35.6 7.2 %all-to-all-start = ((bf16[16,128,128]{2,0,1:T(8,128)(2,1)}), bf16[16,128,128]{2,0,1:T(8,128)(2,1)S(1)}, u32[]{:S(2)}, u32[]{:S(2)}) async-start(bf16[16,128,128]{2,0,1:T(8,128)(2,1)} %bitcast.11), calls=%async_computation | async-start | bytes 1048576 | tf_op jit(solution)/shard_map/all_to_all | solution.py:112
  43.7 32.1 %all-to-all-done = bf16[16,128,128]{2,0,1:T(8,128)(2,1)S(1)} async-done(((bf16[16,128,128]{2,0,1:T(8,128)(2,1)}), bf16[16,128,128]{2,0,1:T(8,128)(2,1)S(1)}, u32[]{:S(2)}, u32[]{:S(2)}) %all-to-all-start) | async-done | bytes 524320 | tf_op jit(solution)/shard_map/all_to_all | solution.py:112
  75.8 18.8 %while.14 = (s32[]{:T(128)}, f32[1,128]{1,0:T(1,128)S(1)}, f32[1,128]{1,0:T(1,128)S(1)}, f32[128,1,64]{0,2,1:T(8,128)S(1)}, s32[]{:T(128)}, /*index=5*/s32[]{:T(...) while((s32[]{:T(128)}, f32[1,128]{1,0:T(1,128)S(1)}, ...), condition=%wide.region_3.4_spmd, body=%wide.region_0.3_spmd.sunk | while | flops 4326023 | bytes 353099 | solution.py:123
  75.8 0.7 add_compare_fusion.2
  77.0 0.7 add_compare_fusion.2
  79.3 0.7 add_compare_fusion.2
  80.5 0.7 add_compare_fusion.2
  81.7 0.7 add_compare_fusion.2
  82.9 0.7 add_compare_fusion.2
  85.2 0.7 add_compare_fusion.2
  94.6 0.7 copy.28
  95.4 7.2 %all-to-all-start.2 = ((bf16[128,1,1,64]{3,2,1,0:T(2,128)(2,1)}), bf16[128,1,1,64]{3,2,1,0:T(2,128)(2,1)S(1)}, u32[]{:S(2)}, u32[]{:S(2)}) async-start(bf16[128,1,1,64]{3,2,1,0:T(2,128)(2,1)} %copy.28), calls=%async_computation.2 | async-start | bytes 131072 | tf_op jit(solution)/shard_map/all_to_all | solution.py:126
  102.6 13.4 %all-to-all-done.2 = bf16[128,1,1,64]{3,2,1,0:T(2,128)(2,1)S(1)} async-done(((bf16[128,1,1,64]{3,2,1,0:T(2,128)(2,1)}), bf16[128,1,1,64]{3,2,1,0:T(2,128)(2,1)S(1)}, u32[]{:S(2)}, u32[]{:S(2)}) %all-to-all-start.2) | async-done | bytes 16416 | tf_op jit(solution)/shard_map/all_to_all | solution.py:126
  116.3 1.6 %fusion.94 = (f32[16]{0:T(128)S(1)}, f32[16,1024]{1,0:T(8,128)S(1)}) fusion(bf16[16,512]{1,0:T(8,128)(2,1)S(1)} %reshape.93, bf16[512,1024]{1,0:T(8,128)(2,1)} %param.20, f32[16]{0:T(128)S(1)} %compare_convert_fusion, bf16[16,1024]{1,0:T(8,128)(2,1)S(1)} %copy-done.2), kind=kOutput, calls=%fused_computation.148 | convolution fusion | flops 16842736 | bytes 1163392 | tf_op jit(solution)/shard_map/dot_general | solution.py:134
  118.7 4.3 %collective-permute-start = (bf16[15,512]{1,0:T(8,128)(2,1)S(1)}, bf16[15,512]{1,0:T(8,128)(2,1)S(1)}, u32[]{:S(2)}, u32[]{:S(2)}) collective-permute-start(bf16[15,512]{1,0:T(8,128)(2,1)S(1)} %get-tuple-element.126), channel_id=1, source_target_pairs={{0,4},{4,8},{8,12},{12,16},{16,20},{20,24},{24,28},{28,32},{32,36}... | collective-permute-start | bytes 46088 | tf_op jit(solution)/shard_map/ppermute | solution.py:16
  123.0 1.9 %collective-permute-start.1 = (bf16[15,512]{1,0:T(8,128)(2,1)S(1)}, bf16[15,512]{1,0:T(8,128)(2,1)S(1)}, u32[]{:S(2)}, u32[]{:S(2)}) collective-permute-start(bf16[15,512]{1,0:T(8,128)(2,1)S(1)} %get-tuple-element.127), channel_id=1, source_target_pairs={{4,0},{8,4},{12,8},{16,12},{20,16},{24,20},{28,24},{32,28},{36,32}... | collective-permute-start | bytes 46088 | tf_op jit(solution)/shard_map/ppermute | solution.py:19
  125.0 5.2 %collective-permute-done.1 = bf16[15,512]{1,0:T(8,128)(2,1)S(1)} collective-permute-done((bf16[15,512]{1,0:T(8,128)(2,1)S(1)}, bf16[15,512]{1,0:T(8,128)(2,1)S(1)}, u32[]{:S(2)}, u32[]{:S(2)}) %collective-permute-start.1) | collective-permute-done | bytes 15392 | tf_op jit(solution)/shard_map/ppermute | solution.py:19
  130.2 2.3 %fusion.11 = bf16[16,1024]{1,0:T(8,128)(2,1)} fusion(f32[16,1024]{1,0:T(8,128)S(1)} %get-tuple-element.129, bf16[512,1024]{1,0:T(8,128)(2,1)} %param.27, f32[46,512]{1,0:T(8,128)S(1)} %maximum_convert_fusion, f32[512]{0:T(512)S(1)} %copy-done.5, f32[512]{0:T(512)S(1)} %copy-done.6, f32[512]{0:T(512)S(1)} %bitcast.128, f32[512]{0:T(512)S(1)} %bitcast.129, ...), kind=kOutput, calls=%fused_computation.21 | convolution fusion | flops 17367040 | bytes 2230272 | tf_op jit(solution)/shard_map/dot_general | solution.py:146
  (140 shorter events, 14.9 us)
Async XLA Ops:
  0.0 118.1 %copy-start = (bf16[1024,1024]{1,0:T(8,128)(2,1)S(1)}, bf16[1024,1024]{1,0:T(8,128)(2,1)}, u32[]{:S(2)}) copy-start(bf16[1024,1024]{1,0:T(8,128)(2,1)} %param.23) | copy-start | bytes 6291460
  0.0 43.5 %copy-start.1 = (f32[31,512]{1,0:T(8,128)S(1)}, f32[31,512]{1,0:T(8,128)}, u32[]{:S(2)}) copy-start(f32[31,512]{1,0:T(8,128)} %param.24) | copy-start | bytes 190468
  1.6 33.1 %all-to-all-start.1 = ((bf16[1,128,64]{2,0,1:T(2,128)(2,1)}), bf16[1,128,64]{2,0,1:T(2,128)(2,1)S(1)}, u32[]{:S(2)}, u32[]{:S(2)}) async-start(bf16[1,128,64]{2,0,1:T(2,128)(2,1)} %reshape.94), calls=%async_computation.1 | async-start | bytes 131072 | tf_op jit(solution)/shard_map/all_to_all | solution.py:94
  23.0 93.3 %copy-start.2 = (bf16[16,1024]{1,0:T(8,128)(2,1)S(1)}, bf16[16,1024]{1,0:T(8,128)(2,1)}, u32[]{:S(2)}) copy-start(bf16[16,1024]{1,0:T(8,128)(2,1)} %param.18) | copy-start | bytes 98308
  35.6 40.2 %all-to-all-start = ((bf16[16,128,128]{2,0,1:T(8,128)(2,1)}), bf16[16,128,128]{2,0,1:T(8,128)(2,1)S(1)}, u32[]{:S(2)}, u32[]{:S(2)}) async-start(bf16[16,128,128]{2,0,1:T(8,128)(2,1)} %bitcast.11), calls=%async_computation | async-start | bytes 1048576 | tf_op jit(solution)/shard_map/all_to_all | solution.py:112
  42.8 75.3 %copy-start.3 = (f32[1024]{0:T(1024)S(1)}, f32[1024]{0:T(1024)}, u32[]{:S(2)}) copy-start(f32[1024]{0:T(1024)} %param.22) | copy-start | bytes 12292
  42.8 75.3 %copy-start.4 = (f32[1024]{0:T(1024)S(1)}, f32[1024]{0:T(1024)}, u32[]{:S(2)}) copy-start(f32[1024]{0:T(1024)} %param.21) | copy-start | bytes 12292
  95.4 34.8 %copy-start.5 = (f32[512]{0:T(512)S(1)}, f32[512]{0:T(512)}, u32[]{:S(2)}) copy-start(f32[512]{0:T(512)} %param.26) | copy-start | bytes 6148
  95.4 34.8 %copy-start.6 = (f32[512]{0:T(512)S(1)}, f32[512]{0:T(512)}, u32[]{:S(2)}) copy-start(f32[512]{0:T(512)} %param.25) | copy-start | bytes 6148
  95.4 20.6 %all-to-all-start.2 = ((bf16[128,1,1,64]{3,2,1,0:T(2,128)(2,1)}), bf16[128,1,1,64]{3,2,1,0:T(2,128)(2,1)S(1)}, u32[]{:S(2)}, u32[]{:S(2)}) async-start(bf16[128,1,1,64]{3,2,1,0:T(2,128)(2,1)} %copy.28), calls=%async_computation.2 | async-start | bytes 131072 | tf_op jit(solution)/shard_map/all_to_all | solution.py:126
  118.7 6.3 %collective-permute-start = (bf16[15,512]{1,0:T(8,128)(2,1)S(1)}, bf16[15,512]{1,0:T(8,128)(2,1)S(1)}, u32[]{:S(2)}, u32[]{:S(2)}) collective-permute-start(bf16[15,512]{1,0:T(8,128)(2,1)S(1)} %get-tuple-element.126), channel_id=1, source_target_pairs={{0,4},{4,8},{8,12},{12,16},{16,20},{20,24},{24,28},{28,32},{32,36}... | collective-permute-start | bytes 46088 | tf_op jit(solution)/shard_map/ppermute | solution.py:16
  123.0 7.2 %collective-permute-start.1 = (bf16[15,512]{1,0:T(8,128)(2,1)S(1)}, bf16[15,512]{1,0:T(8,128)(2,1)S(1)}, u32[]{:S(2)}, u32[]{:S(2)}) collective-permute-start(bf16[15,512]{1,0:T(8,128)(2,1)S(1)} %get-tuple-element.127), channel_id=1, source_target_pairs={{4,0},{8,4},{12,8},{16,12},{20,16},{24,20},{28,24},{32,28},{36,32}... | collective-permute-start | bytes 46088 | tf_op jit(solution)/shard_map/ppermute | solution.py:19
where the time goes:
time: 133 us; the launch traced here: 132 us
  waiting for transfers between devices  62.4 us (47%)
  starting transfers between devices  40.3 us (30%)
  other arithmetic  12.2 us (9%)
  matrix products  10.9 us (8%)
  local copies, waits for them, and re-layouts  5.18 us (4%)
    all_to_all x1, waiting for transfers between devices, on_device(): lax.all_to_all(paired, 'seq', split_axis=1, concat_axis=0, tiled=True)  32.1 us
    all_to_all x1, starting transfers between devices, on_device(): lax.all_to_all(queries.reshape(sub_rows, devices, columns), 'seq', split_...  19.7 us
    all_to_all x1, waiting for transfers between devices, on_device(): lax.all_to_all(context.reshape(devices, sub_rows, 1, columns), 'seq', spl...  13.4 us
    all_to_all x1, waiting for transfers between devices, on_device(): lax.all_to_all(queries.reshape(sub_rows, devices, columns), 'seq', split_...  11.7 us
    lt x16, other arithmetic, attend(): scores = jnp.where((key_frames < limit)[None, None, :], scores, -1e+30)  10.5 us
    all_to_all x1, starting transfers between devices, on_device(): lax.all_to_all(context.reshape(devices, sub_rows, 1, columns), 'seq', spl...  7.21 us
    all_to_all x1, starting transfers between devices, on_device(): lax.all_to_all(paired, 'seq', split_axis=1, concat_axis=0, tiled=True)  7.2 us
    ppermute x1, waiting for transfers between devices, extended(): lax.ppermute(lax.slice_in_dim(block, 0, width, axis=dim), axis, backward)  5.2 us
  transfers between devices with their start and end apart: 5, of which 4 were waited for; matrix products, arithmetic and copies ran while one was open for 1% of the time, Pallas kernels for 0%

commit v1 on v0

v1 whole, which is shorter than its diff:
```python
import functools
import math

import jax
import jax.numpy as jnp
from jax import lax
from jax.experimental import pallas as pl
from jax.experimental.pallas import tpu as pltpu
from jax.sharding import PartitionSpec as P

MESH = pl.DeviceIdType.MESH
BF16 = jnp.bfloat16
F32 = jnp.float32

NZ = 16
SLAB = 8
ROWS = 16
HALF = 256
HEAD = 64


def slot_of(offset):
    return 2 * abs(offset) - (1 if offset > 0 else 0)


FIRST = (4, -4, 3, -3)
NEAR = (2, -2, 1, -1)
RELAYS = ((-4, 4), (-3, 4), (3, -4), (-4, 2), (4, -2), (-3, 2), (3, -2))


def landed(offset):
    return 15 if offset in (8, -8) else slot_of(offset)


def kernel(
    q_hbm, k_hbm, v_hbm, res_hbm, len_ref, wo_hbm, gain_hbm, bias_hbm, wi_hbm, taps_hbm, scale_hbm, shift_hbm, wc_hbm,
    out_ref,
    q_in, k_in, v_in, res, wo, gain, bias, wi, taps, scale, shift, wc,
    kv_own, kv, q_own, q_all, a_send, a_recv, ctx_own, ctx, gated,
    in_sem, kv_ss, kv_rs, q_ss, q_rs, r_ss, r_rs, a_ss, a_rs, c_ss, c_rs,
):
    me = lax.axis_index("seq")
    z = me // SLAB
    xc = lax.rem(me, SLAB)
    par = lax.rem(z, 2)
    other = 1 - par
    limit = len_ref[0]

    def at_z(offset):
        return lax.rem(z + offset + NZ, NZ) * SLAB + xc

    def at_slab(step):
        return z * SLAB + lax.rem(xc + step, SLAB)

    partner = (z + 1 - 2 * par) * SLAB + xc
    left = lax.rem(me + 127, 128)
    right = lax.rem(me + 1, 128)

    loads = [
        pltpu.make_async_copy(src, dst, in_sem.at[i])
        for i, (src, dst) in enumerate(
            (
                (k_hbm, k_in), (v_hbm, v_in), (q_hbm, q_in), (res_hbm, res.at[1]),
                (wo_hbm, wo), (wi_hbm, wi), (wc_hbm, wc),
                (gain_hbm, gain), (bias_hbm, bias), (taps_hbm, taps), (scale_hbm, scale), (shift_hbm, shift),
            )
        )
    ]
    for load in loads[:4]:
        load.start()

    barrier = pltpu.get_barrier_semaphore()
    greet = [at_z(d) for d in FIRST + NEAR] + [at_slab(i) for i in range(1, SLAB)] + [left, right]
    for target in greet:
        pl.semaphore_signal(barrier, inc=1, device_id={"seq": target}, device_id_type=MESH)
    for load in loads[4:]:
        load.start()
    for load in loads[:3]:
        load.wait()
    for g in range(2):
        kv_own[g, 0] = k_in[:, HALF * g : HALF * (g + 1)]
        kv_own[g, 1] = v_in[:, HALF * g : HALF * (g + 1)]
        q_own[g] = q_in[:, HALF * g : HALF * (g + 1)]
    kv[0] = kv_own[par]
    q_all[xc, par] = q_own[par]
    loads[3].wait()
    pl.semaphore_wait(barrier, len(greet))

    def remote(src, dst, ss, rs, target):
        return pltpu.make_async_remote_copy(
            src_ref=src, dst_ref=dst, send_sem=ss, recv_sem=rs, device_id={"seq": target}, device_id_type=MESH
        )

    def first(d):
        slot = slot_of(-d)
        g = lax.rem(par + abs(d), 2)
        return remote(kv_own.at[g], kv.at[slot], kv_ss.at[slot], kv_rs.at[slot], at_z(d))

    def relay(source, d):
        slot = landed(source - d)
        return remote(kv.at[slot_of(source)], kv.at[slot], kv_ss.at[slot], kv_rs.at[slot], at_z(d))

    def arrived(slot):
        remote(kv.at[slot], kv.at[slot], kv_ss.at[slot], kv_rs.at[slot], right).wait_recv()

    first_copies = [first(d) for d in FIRST + NEAR]
    q_first = remote(q_own.at[other], q_all.at[xc, par], q_ss.at[0], q_rs.at[0], partner)
    for copy in first_copies[:4]:
        copy.start()
    q_first.start()
    for copy in first_copies[4:]:
        copy.start()

    remote(q_own.at[other], q_all.at[xc, other], q_ss.at[0], q_rs.at[0], partner).wait_recv()
    q_copies = [
        remote(q_all.at[xc], q_all.at[xc], q_ss.at[i], q_rs.at[i], at_slab(i)) for i in range(1, SLAB)
    ]
    for copy in q_copies:
        copy.start()
    res_right = remote(res.at[1], res.at[0], r_ss.at[0], r_rs.at[0], right)
    res_left = remote(res.at[1], res.at[2], r_ss.at[1], r_rs.at[1], left)
    res_right.start()
    res_left.start()

    relay_copies = []
    seen = []
    for source, d in RELAYS:
        if source not in seen:
            arrived(slot_of(source))
            seen.append(source)
        copy = relay(source, d)
        copy.start()
        relay_copies.append(copy)

    for i in range(1, SLAB):
        sender = lax.rem(xc + SLAB - i, SLAB)
        remote(q_all.at[sender], q_all.at[sender], q_ss.at[i], q_rs.at[i], at_slab(i)).wait_recv()
    for offset in (1, -1, 2, -2):
        arrived(slot_of(offset))

    lane = lax.broadcasted_iota(jnp.int32, (1, 128), 1)
    low = lane < HEAD
    factor = 1.0 / math.sqrt(HEAD)

    queries = []
    for pair in range(2):
        tile = q_all[:, :, :, 128 * pair : 128 * (pair + 1)].reshape(256, 128) * jnp.asarray(factor, BF16)
        zero = jnp.zeros_like(tile)
        queries.append((jnp.where(low, tile, zero), jnp.where(low, zero, tile)))

    def chunk(part):
        slot = 8 * part + lane // ROWS
        away = (slot + 1) // 2
        offset = jnp.where(lax.rem(slot, 2) == 1, away, -away)
        source = lax.rem(z + offset + NZ, NZ)
        frame = (source * SLAB + xc) * ROWS + lax.rem(lane, ROWS)
        valid = frame < limit
        result = []
        for pair in range(2):
            cols = slice(128 * pair, 128 * (pair + 1))
            key = kv[8 * part : 8 * part + 8, 0, :, cols].reshape(128, 128)
            value = kv[8 * part : 8 * part + 8, 1, :, cols].reshape(128, 128)
            for half in range(2):
                scores = lax.dot_general(
                    queries[pair][half], key, (((1,), (1,)), ((), ())), preferred_element_type=F32
                )
                scores = jnp.where(valid, scores, -1e30)
                top = jnp.max(scores, axis=-1, keepdims=True)
                powered = jnp.exp(scores - top)
                total = jnp.sum(powered, axis=-1, keepdims=True)
                mixed_values = jnp.dot(powered.astype(BF16), value, preferred_element_type=F32)
                result.append((top, total, mixed_values))
        return result

    near = chunk(0)
    arrived(slot_of(-4)) if -4 not in seen else None
    for slot in range(9, 16):
        arrived(slot)
    far = chunk(1)

    stats = jnp.zeros((256, 128), F32)
    for pair in range(2):
        tiles = []
        for half in range(2):
            head = 2 * pair + half
            top_a, total_a, mixed_a = near[head]
            top_b, total_b, mixed_b = far[head]
            top = jnp.maximum(top_a, top_b)
            grow_a = jnp.exp(top_a - top)
            grow_b = jnp.exp(top_b - top)
            total = grow_a * total_a + grow_b * total_b
            inverse = 1.0 / total
            tiles.append((grow_a * inverse) * mixed_a + (grow_b * inverse) * mixed_b)
            level = top + jnp.log(total)
            for step in range(3):
                rounded = level.astype(BF16).astype(F32)
                stats = jnp.where(lane == 3 * head + step, rounded, stats)
                level = level - rounded
        a_send[:, 128 * pair : 128 * (pair + 1)] = jnp.where(low, tiles[0], tiles[1]).astype(BF16)
    a_send[:, HALF : HALF + 128] = stats.astype(BF16)

    a_copies = []
    for i in range(1, SLAB):
        owner = lax.rem(xc + i, SLAB)
        copy = remote(
            a_send.at[pl.ds(pl.multiple_of(owner * 32, 32), 32)], a_recv.at[xc], a_ss.at[i], a_rs.at[i], at_slab(i)
        )
        copy.start()
        a_copies.append(copy)
    a_recv[xc] = a_send[pl.ds(pl.multiple_of(xc * 32, 32), 32), :]
    row_id = lax.broadcasted_iota(jnp.int32, (128, HALF), 0)
    col_id = lax.broadcasted_iota(jnp.int32, (128, HALF), 1)
    spread = jnp.where(row_id // 3 == col_id // HEAD, 1.0, 0.0).astype(BF16)
    for i in range(1, SLAB):
        sender = lax.rem(xc + SLAB - i, SLAB)
        remote(a_recv.at[sender], a_recv.at[sender], a_ss.at[i], a_rs.at[i], at_slab(i)).wait_recv()
    parts = a_recv[:, :, :HALF].astype(F32)
    levels = jnp.dot(
        a_recv[:, :, HALF : HALF + 128].reshape(256, 128), spread, preferred_element_type=F32
    ).reshape(8, 32, HALF)
    weights = jnp.exp(levels - jnp.max(levels, axis=0, keepdims=True))
    context = jnp.sum(weights * parts, axis=0) / jnp.sum(weights, axis=0)
    ctx_own[...] = context.astype(BF16).reshape(2, ROWS, HALF)

    c_copies = []
    for where, (slab, start) in enumerate(((par, me), (other, partner))):
        for place, shift_by in ((0, 1), (2, 127), (1, 0)):
            if where == 0 and place == 1:
                continue
            target = lax.rem(start + shift_by, 128)
            copy = remote(
                ctx_own.at[slab], ctx.at[par, place], c_ss.at[where, place], c_rs.at[par, place], target
            )
            copy.start()
            c_copies.append(copy)
    ctx[par, 1] = ctx_own[par]

    for load in loads[4:]:
        load.wait()
    for place in (0, 2):
        for g in range(2):
            remote(ctx.at[g, place], ctx.at[g, place], c_ss.at[0, place], c_rs.at[g, place], right).wait_recv()
    remote(ctx.at[other, 1], ctx.at[other, 1], c_ss.at[1, 1], c_rs.at[other, 1], right).wait_recv()
    remote(res.at[1], res.at[0], r_ss.at[0], r_rs.at[0], right).wait_recv()
    remote(res.at[1], res.at[2], r_ss.at[1], r_rs.at[1], left).wait_recv()

    frames = (me - 1) * ROWS + lax.broadcasted_iota(jnp.int32, (48, 1), 0)
    inside = jnp.where((frames >= 0) & (frames < limit), 1.0, 0.0)
    projected = jnp.dot(ctx[0].reshape(48, HALF), wo[:HALF], preferred_element_type=F32) + jnp.dot(
        ctx[1].reshape(48, HALF), wo[HALF:], preferred_element_type=F32
    )
    mixed = res[...].reshape(48, 1024).astype(F32) + inside * projected
    average = jnp.mean(mixed, axis=-1, keepdims=True)
    centred = mixed - average
    variance = jnp.mean(centred * centred, axis=-1, keepdims=True)
    normed = (centred * lax.rsqrt(variance + 1e-05) * gain[...] + bias[...]).astype(BF16)
    lifted = jnp.dot(normed, wi[...], preferred_element_type=F32)
    gated[...] = (
        (inside * lifted[:, :512] * jax.nn.sigmoid(lifted[:, 512:])).astype(BF16).astype(F32)
    )
    filtered = taps[0:1, :] * gated[1 : 1 + ROWS, :]
    for tap in range(1, 31):
        filtered = filtered + taps[tap : tap + 1, :] * gated[tap + 1 : tap + 1 + ROWS, :]
    shifted = filtered * scale[...] + shift[...]
    activated = (shifted * jax.nn.sigmoid(shifted)).astype(BF16)
    out_ref[...] = (mixed[ROWS : 2 * ROWS] + jnp.dot(activated, wc[...], preferred_element_type=F32)).astype(BF16)

    for copy in first_copies + relay_copies + [q_first] + q_copies + [res_right, res_left] + a_copies + c_copies:
        copy.wait_send()


def on_device(
    queries, keys, values, residual, lengths, out_proj, ln_gain, ln_bias, conv_in, taps, bn_scale, bn_shift, conv_out
):
    hbm = pl.BlockSpec(memory_space=pl.ANY)
    dma = pltpu.SemaphoreType.DMA
    return pl.pallas_call(
        kernel,
        out_shape=jax.ShapeDtypeStruct((ROWS, 1024), BF16),
        in_specs=[hbm] * 4 + [pl.BlockSpec(memory_space=pltpu.SMEM)] + [hbm] * 8,
        out_specs=pl.BlockSpec(memory_space=pltpu.VMEM),
        scratch_shapes=[
            pltpu.VMEM((ROWS, 512), BF16),
            pltpu.VMEM((ROWS, 512), BF16),
            pltpu.VMEM((ROWS, 512), BF16),
            pltpu.VMEM((3, ROWS, 1024), BF16),
            pltpu.VMEM((512, 1024), BF16),
            pltpu.VMEM((1, 1024), F32),
            pltpu.VMEM((1, 1024), F32),
            pltpu.VMEM((1024, 1024), BF16),
            pltpu.VMEM((31, 512), F32),
            pltpu.VMEM((1, 512), F32),
            pltpu.VMEM((1, 512), F32),
            pltpu.VMEM((512, 1024), BF16),
            pltpu.VMEM((2, 2, ROWS, HALF), BF16),
            pltpu.VMEM((NZ, 2, ROWS, HALF), BF16),
            pltpu.VMEM((2, ROWS, HALF), BF16),
            pltpu.VMEM((SLAB, 2, ROWS, HALF), BF16),
            pltpu.VMEM((256, HALF + 128), BF16),
            pltpu.VMEM((SLAB, 32, HALF + 128), BF16),
            pltpu.VMEM((2, ROWS, HALF), BF16),
            pltpu.VMEM((2, 3, ROWS, HALF), BF16),
            pltpu.VMEM((48, 512), F32),
            dma((12,)),
            dma((NZ,)),
            dma((NZ,)),
            dma((SLAB,)),
            dma((SLAB,)),
            dma((2,)),
            dma((2,)),
            dma((SLAB,)),
            dma((SLAB,)),
            dma((2, 3)),
            dma((2, 3)),
        ],
        compiler_params=pltpu.CompilerParams(
            collective_id=0, has_side_effects=True, vmem_limit_bytes=40 * 1024 * 1024
        ),
        name="conformer",
    )(
        queries, keys, values, residual, lengths, out_proj, ln_gain.reshape(1, -1), ln_bias.reshape(1, -1), conv_in,
        taps, bn_scale.reshape(1, -1), bn_shift.reshape(1, -1), conv_out,
    )


def solution(mesh):
    rows = P(("dp", "seq"), None)
    return jax.shard_map(
        on_device,
        mesh=mesh,
        in_specs=(rows, rows, rows, rows, P("dp")) + (P(),) * 8,
        out_specs=rows,
        check_vma=False,
    )
```

time: 133 us -> 47.6 us (0.36)
  the two profiles are of different devices: /device:TPU:31 before, /device:TPU:1 now
where the time goes in v1:
time: 47.6 us; the launch traced here: 47 us
  Pallas kernels  35.2 us (74%)
  local copies, waits for them, and re-layouts  11.1 us (23%)
  between operations  0.68 us (1%)
    pallas_call x1, Pallas kernels, on_device(): pl.pallas_call(kernel, out_shape=jax.ShapeDtypeStruct((ROWS, 1024), BF16)...  35.2 us
    unnamed x25, local copies, waits for them, and re-layouts  11.1 us

profile of v1, /device:TPU:1, one launch (start us, length us, event | category | flops | bytes accessed | tf_op | source)
XLA Modules:
  0.0 47.0 jit_solution(9304010181754446987)
XLA Ops:
  0.7 0.0 copy-start
  0.7 1.6 %copy-done = bf16[1024,1024]{1,0:T(8,128)(2,1)S(1)} copy-done((bf16[1024,1024]{1,0:T(8,128)(2,1)S(1)}, bf16[1024,1024]{1,0:T(8,128)(2,1)}, u32[]{:S(2)}) %copy-start) | copy-done | bytes 2097176
  2.2 1.2 %copy-done.1 = bf16[512,1024]{1,0:T(8,128)(2,1)S(1)} copy-done((bf16[512,1024]{1,0:T(8,128)(2,1)S(1)}, bf16[512,1024]{1,0:T(8,128)(2,1)}, u32[]{:S(2)}) %copy-start.1) | copy-done | bytes 1048600
  3.5 0.0 copy-start.2
  3.5 1.2 %copy-done.2 = bf16[512,1024]{1,0:T(8,128)(2,1)S(1)} copy-done((bf16[512,1024]{1,0:T(8,128)(2,1)S(1)}, bf16[512,1024]{1,0:T(8,128)(2,1)}, u32[]{:S(2)}) %copy-start.2) | copy-done | bytes 1048600
  4.7 0.0 copy-start.3
  4.7 0.8 %copy-done.3 = f32[31,512]{1,0:T(8,128)S(1)} copy-done((f32[31,512]{1,0:T(8,128)S(1)}, f32[31,512]{1,0:T(8,128)}, u32[]{:S(2)}) %copy-start.3) | copy-done | bytes 63512
  5.5 0.0 copy-start.4
  5.5 0.8 %copy-done.4 = bf16[16,1024]{1,0:T(8,128)(2,1)S(1)} copy-done((bf16[16,1024]{1,0:T(8,128)(2,1)S(1)}, bf16[16,1024]{1,0:T(8,128)(2,1)}, u32[]{:S(2)}) %copy-start.4) | copy-done | bytes 32792
  6.3 0.0 copy-start.5
  6.3 0.7 %copy-done.5 = bf16[16,512]{1,0:T(8,128)(2,1)S(1)} copy-done((bf16[16,512]{1,0:T(8,128)(2,1)S(1)}, bf16[16,512]{1,0:T(8,128)(2,1)}, u32[]{:S(2)}) %copy-start.5) | copy-done | bytes 16408
  7.0 0.0 copy-start.6
  7.0 0.7 %copy-done.6 = bf16[16,512]{1,0:T(8,128)(2,1)S(1)} copy-done((bf16[16,512]{1,0:T(8,128)(2,1)S(1)}, bf16[16,512]{1,0:T(8,128)(2,1)}, u32[]{:S(2)}) %copy-start.6) | copy-done | bytes 16408
  7.7 0.0 copy-start.7
  7.7 0.7 %copy-done.7 = bf16[16,512]{1,0:T(8,128)(2,1)S(1)} copy-done((bf16[16,512]{1,0:T(8,128)(2,1)S(1)}, bf16[16,512]{1,0:T(8,128)(2,1)}, u32[]{:S(2)}) %copy-start.7) | copy-done | bytes 16408
  8.4 0.0 copy-start.8
  8.4 0.7 %copy-done.8 = f32[1024]{0:T(1024)S(1)} copy-done((f32[1024]{0:T(1024)S(1)}, f32[1024]{0:T(1024)}, u32[]{:S(2)}) %copy-start.8) | copy-done | bytes 4120
  9.1 0.7 %copy-done.9 = f32[1024]{0:T(1024)S(1)} copy-done((f32[1024]{0:T(1024)S(1)}, f32[1024]{0:T(1024)}, u32[]{:S(2)}) %copy-start.9) | copy-done | bytes 4120
  9.8 0.0 copy-start.10
  9.8 0.7 %copy-done.10 = f32[512]{0:T(512)S(1)} copy-done((f32[512]{0:T(512)S(1)}, f32[512]{0:T(512)}, u32[]{:S(2)}) %copy-start.10) | copy-done | bytes 2072
  10.5 0.0 copy-start.11
  10.5 0.7 %copy-done.11 = f32[512]{0:T(512)S(1)} copy-done((f32[512]{0:T(512)S(1)}, f32[512]{0:T(512)}, u32[]{:S(2)}) %copy-start.11) | copy-done | bytes 2072
  11.2 35.2 %conformer.1 = bf16[16,1024]{1,0:T(8,128)(2,1)S(1)} custom-call(bf16[16,512]{1,0:T(8,128)(2,1)S(1)} %copy-done.5, bf16[16,512]{1,0:T(8,128)(2,1)S(1)} %copy-done.6, bf16[16,512]{1,0:T(8,128)(2,1)S(1)} %copy-done.7, bf16[16,1024]{1,0:T(8,128)(2,1)S(1)} %copy-done.4, s32[1]{0:T(128)S(6)} %copy.15.len_ref, bf16[512,1024]{1,0:T(8,128)(2,1)S(1)} %copy-done.1, ...), custom_call_target="tpu_custom_call" | custom-call | tf_op jit(solution)/shard_map/conformer/pallas_call | solution.py:277
  46.3 0.6 %copy.16 = bf16[16,1024]{1,0:T(8,128)(2,1)} copy(bf16[16,1024]{1,0:T(8,128)(2,1)S(1)} %conformer.1) | data formatting | bytes 65536
  (2 shorter events, 0.0 us)
Async XLA Ops:
  0.7 1.6 %copy-start = (bf16[1024,1024]{1,0:T(8,128)(2,1)S(1)}, bf16[1024,1024]{1,0:T(8,128)(2,1)}, u32[]{:S(2)}) copy-start(bf16[1024,1024]{1,0:T(8,128)(2,1)} %wi_hbm.1) | copy-start | bytes 6291460
  2.2 1.2 %copy-start.1 = (bf16[512,1024]{1,0:T(8,128)(2,1)S(1)}, bf16[512,1024]{1,0:T(8,128)(2,1)}, u32[]{:S(2)}) copy-start(bf16[512,1024]{1,0:T(8,128)(2,1)} %wo_hbm.1) | copy-start | bytes 3145732
  3.5 1.2 %copy-start.2 = (bf16[512,1024]{1,0:T(8,128)(2,1)S(1)}, bf16[512,1024]{1,0:T(8,128)(2,1)}, u32[]{:S(2)}) copy-start(bf16[512,1024]{1,0:T(8,128)(2,1)} %wc_hbm.1) | copy-start | bytes 3145732
  4.7 0.8 %copy-start.3 = (f32[31,512]{1,0:T(8,128)S(1)}, f32[31,512]{1,0:T(8,128)}, u32[]{:S(2)}) copy-start(f32[31,512]{1,0:T(8,128)} %taps_hbm.1) | copy-start | bytes 190468
  5.5 0.8 %copy-start.4 = (bf16[16,1024]{1,0:T(8,128)(2,1)S(1)}, bf16[16,1024]{1,0:T(8,128)(2,1)}, u32[]{:S(2)}) copy-start(bf16[16,1024]{1,0:T(8,128)(2,1)} %res_hbm.1) | copy-start | bytes 98308
  6.3 0.7 %copy-start.5 = (bf16[16,512]{1,0:T(8,128)(2,1)S(1)}, bf16[16,512]{1,0:T(8,128)(2,1)}, u32[]{:S(2)}) copy-start(bf16[16,512]{1,0:T(8,128)(2,1)} %q_hbm.1) | copy-start | bytes 49156
  7.0 0.7 %copy-start.6 = (bf16[16,512]{1,0:T(8,128)(2,1)S(1)}, bf16[16,512]{1,0:T(8,128)(2,1)}, u32[]{:S(2)}) copy-start(bf16[16,512]{1,0:T(8,128)(2,1)} %k_hbm.1) | copy-start | bytes 49156
  7.7 0.7 %copy-start.7 = (bf16[16,512]{1,0:T(8,128)(2,1)S(1)}, bf16[16,512]{1,0:T(8,128)(2,1)}, u32[]{:S(2)}) copy-start(bf16[16,512]{1,0:T(8,128)(2,1)} %v_hbm.1) | copy-start | bytes 49156
  8.4 0.7 %copy-start.8 = (f32[1024]{0:T(1024)S(1)}, f32[1024]{0:T(1024)}, u32[]{:S(2)}) copy-start(f32[1024]{0:T(1024)} %param.19) | copy-start | bytes 12292
  9.1 0.7 %copy-start.9 = (f32[1024]{0:T(1024)S(1)}, f32[1024]{0:T(1024)}, u32[]{:S(2)}) copy-start(f32[1024]{0:T(1024)} %param.20) | copy-start | bytes 12292
  9.8 0.7 %copy-start.10 = (f32[512]{0:T(512)S(1)}, f32[512]{0:T(512)}, u32[]{:S(2)}) copy-start(f32[512]{0:T(512)} %param.23) | copy-start | bytes 6148
  10.5 0.7 %copy-start.11 = (f32[512]{0:T(512)S(1)}, f32[512]{0:T(512)}, u32[]{:S(2)}) copy-start(f32[512]{0:T(512)} %param.24) | copy-start | bytes 6148

commit v2 on v1

--- a/solution.py
+++ b/solution.py
@@ -272,7 +272,7 @@
 def on_device(
     queries, keys, values, residual, lengths, out_proj, ln_gain, ln_bias, conv_in, taps, bn_scale, bn_shift, conv_out
 ):
-    hbm = pl.BlockSpec(memory_space=pl.ANY)
+    hbm = pl.BlockSpec(memory_space=pltpu.HBM)
     dma = pltpu.SemaphoreType.DMA
     return pl.pallas_call(
         kernel,
@@ -318,8 +318,8 @@
         ),
         name="conformer",
     )(
-        queries, keys, values, residual, lengths, out_proj, ln_gain.reshape(1, -1), ln_bias.reshape(1, -1), conv_in,
-        taps, bn_scale.reshape(1, -1), bn_shift.reshape(1, -1), conv_out,
+        *[pltpu.with_memory_space_constraint(a, pltpu.HBM) if a is not lengths else a for a in (queries, keys, values, residual, lengths, out_proj, ln_gain.reshape(1, -1), ln_bias.reshape(1, -1), conv_in,
+        taps, bn_scale.reshape(1, -1), bn_shift.reshape(1, -1), conv_out)],
     )
 
 

time: 47.6 us -> 36.5 us (0.77)
  local copies, waits for them, and re-layouts: 11.1 us -> 0.62 us
    unnamed x25 -> x1, local copies, waits for them, and re-layouts: 11.1 us -> 0.62 us
where the time goes in v2:
time: 36.5 us; the launch traced here: 36.3 us
  Pallas kernels  35.1 us (96%)
  between operations  0.66 us (2%)
  local copies, waits for them, and re-layouts  0.62 us (2%)
    pallas_call x1, Pallas kernels, on_device(): pl.pallas_call(kernel, out_shape=jax.ShapeDtypeStruct((ROWS, 1024), BF16)...  35.1 us

profile of v2, /device:TPU:1, one launch (start us, length us, event | category | flops | bytes accessed | tf_op | source)
XLA Modules:
  0.0 36.3 jit_solution(1538904456527383181)
XLA Ops:
  0.7 35.1 %conformer.1 = bf16[16,1024]{1,0:T(8,128)(2,1)S(1)} custom-call(bf16[16,512]{1,0:T(8,128)(2,1)} %q_hbm.1, bf16[16,512]{1,0:T(8,128)(2,1)} %k_hbm.1, bf16[16,512]{1,0:T(8,128)(2,1)} %v_hbm.1, bf16[16,1024]{1,0:T(8,128)(2,1)} %res_hbm.1, s32[1]{0:T(128)S(6)} %copy.15.len_ref, bf16[512,1024]{1,0:T(8,128)(2,1)} %wo_hbm.1, f32[1,1024]{1,0:T(1,128)} %bitcast.4, ...), custom_call_target="tpu_custom_call" | custom-call | tf_op jit(solution)/shard_map/conformer/pallas_call | solution.py:277
  35.7 0.6 %copy.16 = bf16[16,1024]{1,0:T(8,128)(2,1)} copy(bf16[16,1024]{1,0:T(8,128)(2,1)S(1)} %conformer.1) | data formatting | bytes 65536

commit v3 on v2

v3 whole, which is shorter than its diff:
```python
import math

import jax
import jax.numpy as jnp
from jax import lax
from jax.experimental import pallas as pl
from jax.experimental.pallas import tpu as pltpu
from jax.sharding import PartitionSpec as P

MESH = pl.DeviceIdType.MESH
BF16 = jnp.bfloat16
F32 = jnp.float32

NZ = 16
SLAB = 8
ROWS = 16
WIDE = 128
HEAD = 64


def slot_of(offset):
    return 15 if offset in (8, -8) else 2 * abs(offset) - (1 if offset > 0 else 0)


FIRST = (4, -4, 3, -3, 2, -2, 1, -1)
RELAYS = ((-1, 4), (1, -4), (-2, 4), (2, -4), (-3, 4), (3, -4), (-4, 4))


def kernel(
    q_hbm, k_hbm, v_hbm, res_hbm, len_ref, wo_hbm, gain_hbm, bias_hbm, wi_hbm, taps_hbm, scale_hbm, shift_hbm, wc_hbm,
    out_ref,
    q_in, k_in, v_in, res, wo, gain, bias, wi, taps, scale, shift, wc,
    kv_own, kv, q_own, q_all, a_send, a_recv, ctx_own, ctx, gated,
    in_sem, kv_ss, kv_rs, q_ss, q_rs, r_ss, r_rs, a_ss, a_rs, c_ss, c_rs,
):
    me = lax.axis_index("seq")
    z = me // SLAB
    xc = lax.rem(me, SLAB)
    mine = lax.rem(z + 1, 4)
    limit = len_ref[0]

    def at_z(offset):
        return lax.rem(z + offset + NZ, NZ) * SLAB + xc

    def at_slab(step):
        return z * SLAB + lax.rem(xc + step, SLAB)

    def member(place):
        return lax.rem(z - mine + place + NZ, NZ)

    has_left = me != 0
    has_right = me != 127
    left = jnp.maximum(me - 1, 0)
    right = jnp.minimum(me + 1, 127)
    slab_steps = (4, 3, 5, 2, 6, 7, 1)

    barrier = pltpu.get_barrier_semaphore()

    def greet(target):
        pl.semaphore_signal(barrier, inc=1, device_id={"seq": target}, device_id_type=MESH)

    for d in FIRST[:6]:
        greet(at_z(d))
    for step in slab_steps:
        greet(at_slab(step))
    for d in FIRST[6:]:
        greet(at_z(d))

    loads = [
        pltpu.make_async_copy(src, dst, in_sem.at[i])
        for i, (src, dst) in enumerate(
            (
                (k_hbm, k_in), (v_hbm, v_in), (q_hbm, q_in), (res_hbm, res.at[1]),
                (wo_hbm, wo), (wi_hbm, wi), (wc_hbm, wc),
                (gain_hbm, gain), (bias_hbm, bias), (taps_hbm, taps), (scale_hbm, scale), (shift_hbm, shift),
            )
        )
    ]
    for load in loads:
        load.start()
    for load in loads[:3]:
        load.wait()
    for g in range(4):
        cols = slice(WIDE * g, WIDE * (g + 1))
        kv_own[g, 0] = k_in[:, cols]
        kv_own[g, 1] = v_in[:, cols]
        q_own[g] = q_in[:, cols]
    kv[0] = kv_own[mine]
    q_all[xc, mine] = q_own[mine]
    loads[3].wait()
    pl.semaphore_wait(barrier, 15)

    def remote(src, dst, ss, rs, target):
        return pltpu.make_async_remote_copy(
            src_ref=src, dst_ref=dst, send_sem=ss, recv_sem=rs, device_id={"seq": target}, device_id_type=MESH
        )

    def first(d):
        slot = slot_of(-d)
        return remote(
            kv_own.at[lax.rem(mine + d + 4, 4)], kv.at[slot], kv_ss.at[slot], kv_rs.at[slot], at_z(d)
        )

    def relay(source, d):
        slot = slot_of(source - d)
        return remote(kv.at[slot_of(source)], kv.at[slot], kv_ss.at[slot], kv_rs.at[slot], at_z(d))

    def arrived(slot):
        remote(kv.at[slot], kv.at[slot], kv_ss.at[slot], kv_rs.at[slot], right).wait_recv()

    sent = []

    def start(copy):
        copy.start()
        sent.append(copy)

    for d in FIRST[:4]:
        start(first(d))
    for turn in (2, 1, 3):
        place = lax.rem(mine + turn, 4)
        start(
            remote(
                q_own.at[place], q_all.at[xc, mine], q_ss.at[turn], q_rs.at[turn], member(place) * SLAB + xc
            )
        )
    for d in FIRST[4:]:
        start(first(d))
    for source, d in RELAYS[:2]:
        arrived(slot_of(source))
        start(relay(source, d))
    for turn in (2, 1, 3):
        place = lax.rem(mine + 4 - turn, 4)
        remote(q_own.at[0], q_all.at[xc, place], q_ss.at[turn], q_rs.at[turn], right).wait_recv()
    for step in slab_steps:
        start(remote(q_all.at[xc], q_all.at[xc], q_ss.at[4 + step], q_rs.at[4 + step], at_slab(step)))

    for source, d in RELAYS[2:]:
        arrived(slot_of(source))
        start(relay(source, d))

    for step in slab_steps:
        sender = lax.rem(xc + SLAB - step, SLAB)
        remote(q_all.at[sender], q_all.at[sender], q_ss.at[4 + step], q_rs.at[4 + step], right).wait_recv()
    res_right = remote(res.at[1], res.at[0], r_ss.at[0], r_rs.at[0], right)
    res_left = remote(res.at[1], res.at[2], r_ss.at[1], r_rs.at[1], left)
    pl.when(has_right)(res_right.start)
    pl.when(has_left)(res_left.start)
    arrived(slot_of(4))

    lane = lax.broadcasted_iota(jnp.int32, (1, WIDE), 1)
    low = lane < HEAD
    tile = q_all[...].reshape(512, WIDE) * jnp.asarray(1.0 / math.sqrt(HEAD), BF16)
    zero = jnp.zeros_like(tile)
    queries = (jnp.where(low, tile, zero), jnp.where(low, zero, tile))

    def chunk(part):
        slot = 8 * part + lane // ROWS
        away = (slot + 1) // 2
        offset = jnp.where(lax.rem(slot, 2) == 1, away, -away)
        source = lax.rem(z + offset + NZ, NZ)
        frame = (source * SLAB + xc) * ROWS + lax.rem(lane, ROWS)
        valid = frame < limit
        key = kv[8 * part : 8 * part + 8, 0].reshape(128, WIDE)
        value = kv[8 * part : 8 * part + 8, 1].reshape(128, WIDE)
        result = []
        for half in range(2):
            scores = lax.dot_general(queries[half], key, (((1,), (1,)), ((), ())), preferred_element_type=F32)
            scores = jnp.where(valid, scores, -1e30)
            top = jnp.max(scores, axis=-1, keepdims=True)
            powered = jnp.exp(scores - top)
            total = jnp.sum(powered, axis=-1, keepdims=True)
            result.append((top, total, jnp.dot(powered.astype(BF16), value, preferred_element_type=F32)))
        return result

    near = chunk(0)
    for slot in range(9, 16):
        arrived(slot)
    far = chunk(1)

    home = 8 * lax.rem(lax.broadcasted_iota(jnp.int32, (512, WIDE), 0) // ROWS, 4)
    wide_lane = lax.broadcasted_iota(jnp.int32, (512, WIDE), 1) - home
    stats = jnp.zeros((512, WIDE), F32)
    tiles = []
    for half in range(2):
        top_a, total_a, values_a = near[half]
        top_b, total_b, values_b = far[half]
        top = jnp.maximum(top_a, top_b)
        grow_a = jnp.exp(top_a - top)
        grow_b = jnp.exp(top_b - top)
        total = grow_a * total_a + grow_b * total_b
        inverse = 1.0 / total
        tiles.append((grow_a * inverse) * values_a + (grow_b * inverse) * values_b)
        level = top + jnp.log(total)
        for step in range(3):
            rounded = level.astype(BF16).astype(F32)
            stats = jnp.where(wide_lane == 3 * half + step, rounded, stats)
            level = level - rounded
    a_send[:, :64] = jnp.where(low, tiles[0], tiles[1]).astype(BF16).reshape(SLAB, 64, WIDE)
    a_send[:, 64:] = jnp.sum(stats.reshape(SLAB, 4, ROWS, WIDE), axis=1).astype(BF16)

    for step in slab_steps:
        owner = lax.rem(xc + step, SLAB)
        start(remote(a_send.at[owner], a_recv.at[xc], a_ss.at[step], a_rs.at[step], at_slab(step)))
    a_recv[xc] = a_send[xc]
    row_id = lax.broadcasted_iota(jnp.int32, (WIDE, WIDE), 0)
    col_id = lax.broadcasted_iota(jnp.int32, (WIDE, WIDE), 1)
    part_id = lax.rem(row_id, 8)
    picks = [
        jnp.where(
            (row_id // 8 == g) & (part_id >= 3 * (col_id // HEAD)) & (part_id < 3 * (col_id // HEAD) + 3), 1.0, 0.0
        ).astype(BF16)
        for g in range(4)
    ]
    for step in slab_steps[::-1]:
        sender = lax.rem(xc + SLAB - step, SLAB)
        remote(a_recv.at[sender], a_recv.at[sender], a_ss.at[step], a_rs.at[step], right).wait_recv()
    packed = a_recv[:, 64:].reshape(SLAB * ROWS, WIDE)
    for g in range(4):
        levels = jnp.dot(packed, picks[g], preferred_element_type=F32).reshape(SLAB, ROWS, WIDE)
        weights = jnp.exp(levels - jnp.max(levels, axis=0, keepdims=True))
        parts = a_recv[:, ROWS * g : ROWS * (g + 1)].astype(F32)
        ctx_own[g] = (jnp.sum(weights * parts, axis=0) / jnp.sum(weights, axis=0)).astype(BF16)

    edges = []
    for slab in (1, 2, 3, 0):
        home_device = member(slab) * SLAB + xc
        for place in (0, 2, 1):
            target = home_device + 1 - place
            if place == 1:
                exists = slab != mine
                target = home_device
            else:
                exists = (target >= 0) & (target < 128)
            copy = remote(
                ctx_own.at[slab], ctx.at[mine, place], c_ss.at[slab, place], c_rs.at[mine, place],
                jnp.clip(target, 0, 127),
            )
            pl.when(exists)(copy.start)
            edges.append((exists, copy))
    ctx[mine, 1] = ctx_own[mine]

    for load in loads[4:]:
        load.wait()
    def ctx_arrived(group, place):
        remote(ctx.at[group, place], ctx.at[group, place], c_ss.at[0, 0], c_rs.at[group, place], right).wait_recv()

    for turn in range(1, 4):
        ctx_arrived(lax.rem(mine + turn, 4), 1)

    def receive_edge(place):
        for group in range(4):
            ctx_arrived(group, place)

    def blank(place):
        res[place] = jnp.zeros((ROWS, 1024), BF16)
        for group in range(4):
            ctx[group, place] = jnp.zeros((ROWS, WIDE), BF16)

    pl.when(has_left)(remote(res.at[1], res.at[0], r_ss.at[0], r_rs.at[0], right).wait_recv)
    pl.when(has_right)(remote(res.at[1], res.at[2], r_ss.at[1], r_rs.at[1], left).wait_recv)
    pl.when(has_left)(lambda: receive_edge(0))
    pl.when(has_right)(lambda: receive_edge(2))
    pl.when(jnp.logical_not(has_left))(lambda: blank(0))
    pl.when(jnp.logical_not(has_right))(lambda: blank(2))

    frames = (me - 1) * ROWS + lax.broadcasted_iota(jnp.int32, (48, 1), 0)
    inside = jnp.where((frames >= 0) & (frames < limit), 1.0, 0.0)
    context = jnp.concatenate([ctx[group].reshape(48, WIDE) for group in range(4)], axis=1)
    projected = jnp.dot(context, wo[...], preferred_element_type=F32)
    mixed = res[...].reshape(48, 1024).astype(F32) + inside * projected
    average = jnp.mean(mixed, axis=-1, keepdims=True)
    centred = mixed - average
    variance = jnp.mean(centred * centred, axis=-1, keepdims=True)
    normed = (centred * lax.rsqrt(variance + 1e-05) * gain[...] + bias[...]).astype(BF16)
    lifted = jnp.dot(normed, wi[...], preferred_element_type=F32)
    gated[...] = (inside * lifted[:, :512] * jax.nn.sigmoid(lifted[:, 512:])).astype(BF16).astype(F32)
    filtered = taps[0:1, :] * gated[1 : 1 + ROWS, :]
    for tap in range(1, 31):
        filtered = filtered + taps[tap : tap + 1, :] * gated[tap + 1 : tap + 1 + ROWS, :]
    shifted = filtered * scale[...] + shift[...]
    activated = (shifted * jax.nn.sigmoid(shifted)).astype(BF16)
    out_ref[...] = (mixed[ROWS : 2 * ROWS] + jnp.dot(activated, wc[...], preferred_element_type=F32)).astype(BF16)

    for copy in sent:
        copy.wait_send()
    pl.when(has_right)(res_right.wait_send)
    pl.when(has_left)(res_left.wait_send)
    for exists, copy in edges:
        pl.when(exists)(copy.wait_send)


def on_device(
    queries, keys, values, residual, lengths, out_proj, ln_gain, ln_bias, conv_in, taps, bn_scale, bn_shift, conv_out
):
    hbm = pl.BlockSpec(memory_space=pltpu.HBM)
    dma = pltpu.SemaphoreType.DMA

    def stay(array):
        return pltpu.with_memory_space_constraint(array, pltpu.HBM)

    def row(array):
        return stay(array.reshape(1, -1))

    return pl.pallas_call(
        kernel,
        out_shape=jax.ShapeDtypeStruct((ROWS, 1024), BF16),
        in_specs=[hbm] * 4 + [pl.BlockSpec(memory_space=pltpu.SMEM)] + [hbm] * 8,
        out_specs=pl.BlockSpec(memory_space=pltpu.VMEM),
        scratch_shapes=[
            pltpu.VMEM((ROWS, 512), BF16),
            pltpu.VMEM((ROWS, 512), BF16),
            pltpu.VMEM((ROWS, 512), BF16),
            pltpu.VMEM((3, ROWS, 1024), BF16),
            pltpu.VMEM((512, 1024), BF16),
            pltpu.VMEM((1, 1024), F32),
            pltpu.VMEM((1, 1024), F32),
            pltpu.VMEM((1024, 1024), BF16),
            pltpu.VMEM((31, 512), F32),
            pltpu.VMEM((1, 512), F32),
            pltpu.VMEM((1, 512), F32),
            pltpu.VMEM((512, 1024), BF16),
            pltpu.VMEM((4, 2, ROWS, WIDE), BF16),
            pltpu.VMEM((NZ, 2, ROWS, WIDE), BF16),
            pltpu.VMEM((4, ROWS, WIDE), BF16),
            pltpu.VMEM((SLAB, 4, ROWS, WIDE), BF16),
            pltpu.VMEM((SLAB, 80, WIDE), BF16),
            pltpu.VMEM((SLAB, 80, WIDE), BF16),
            pltpu.VMEM((4, ROWS, WIDE), BF16),
            pltpu.VMEM((4, 3, ROWS, WIDE), BF16),
            pltpu.VMEM((48, 512), F32),
            dma((12,)),
            dma((NZ,)),
            dma((NZ,)),
            dma((12,)),
            dma((12,)),
            dma((2,)),
            dma((2,)),
            dma((SLAB,)),
            dma((SLAB,)),
            dma((4, 3)),
            dma((4, 3)),
        ],
        compiler_params=pltpu.CompilerParams(
            collective_id=0, has_side_effects=True, vmem_limit_bytes=40 * 1024 * 1024
        ),
        name="conformer",
    )(
        stay(queries), stay(keys), stay(values), stay(residual), lengths, stay(out_proj), row(ln_gain), row(ln_bias),
        stay(conv_in), stay(taps), row(bn_scale), row(bn_shift), stay(conv_out),
    )


def solution(mesh):
    rows = P(("dp", "seq"), None)
    return jax.shard_map(
        on_device,
        mesh=mesh,
        in_specs=(rows, rows, rows, rows, P("dp")) + (P(),) * 8,
        out_specs=rows,
        check_vma=False,
    )
```

time: 36.5 us -> 35.5 us (0.973)
  Pallas kernels: 35.1 us -> 34.1 us
    pallas_call x1, Pallas kernels: 35.1 us -> 34.1 us  [on_device(): pl.pallas_call(kernel, out_shape=jax.ShapeDtypeStruct((ROWS, 1024), BF16)...]
where the time goes in v3:
time: 35.5 us; the launch traced here: 35.3 us
  Pallas kernels  34.1 us (96%)
  between operations  0.66 us (2%)
  local copies, waits for them, and re-layouts  0.62 us (2%)
    pallas_call x1, Pallas kernels, on_device(): pl.pallas_call(kernel, out_shape=jax.ShapeDtypeStruct((ROWS, 1024), BF16)...  34.1 us

profile of v3, /device:TPU:1, one launch (start us, length us, event | category | flops | bytes accessed | tf_op | source)
XLA Modules:
  0.0 35.3 jit_solution(4732553365221472105)
XLA Ops:
  0.7 34.1 %conformer.1 = bf16[16,1024]{1,0:T(8,128)(2,1)S(1)} custom-call(bf16[16,512]{1,0:T(8,128)(2,1)} %q_hbm.1, bf16[16,512]{1,0:T(8,128)(2,1)} %k_hbm.1, bf16[16,512]{1,0:T(8,128)(2,1)} %v_hbm.1, bf16[16,1024]{1,0:T(8,128)(2,1)} %res_hbm.1, s32[1]{0:T(128)S(6)} %copy.15.len_ref, bf16[512,1024]{1,0:T(8,128)(2,1)} %wo_hbm.1, f32[1,1024]{1,0:T(1,128)} %bitcast.4, ...), custom_call_target="tpu_custom_call" | custom-call | tf_op jit(solution)/shard_map/conformer/pallas_call | solution.py:304
  34.7 0.6 %copy.16 = bf16[16,1024]{1,0:T(8,128)(2,1)} copy(bf16[16,1024]{1,0:T(8,128)(2,1)S(1)} %conformer.1) | data formatting | bytes 65536

commit v4 on v3

--- a/solution.py
+++ b/solution.py
@@ -114,8 +114,6 @@
         copy.start()
         sent.append(copy)
 
-    for d in FIRST[:4]:
-        start(first(d))
     for turn in (2, 1, 3):
         place = lax.rem(mine + turn, 4)
         start(
@@ -123,9 +121,9 @@
                 q_own.at[place], q_all.at[xc, mine], q_ss.at[turn], q_rs.at[turn], member(place) * SLAB + xc
             )
         )
-    for d in FIRST[4:]:
+    for d in FIRST:
         start(first(d))
-    for source, d in RELAYS[:2]:
+    for source, d in RELAYS[:4]:
         arrived(slot_of(source))
         start(relay(source, d))
     for turn in (2, 1, 3):
@@ -134,17 +132,13 @@
     for step in slab_steps:
         start(remote(q_all.at[xc], q_all.at[xc], q_ss.at[4 + step], q_rs.at[4 + step], at_slab(step)))
 
-    for source, d in RELAYS[2:]:
+    for source, d in RELAYS[4:]:
         arrived(slot_of(source))
         start(relay(source, d))
 
     for step in slab_steps:
         sender = lax.rem(xc + SLAB - step, SLAB)
         remote(q_all.at[sender], q_all.at[sender], q_ss.at[4 + step], q_rs.at[4 + step], right).wait_recv()
-    res_right = remote(res.at[1], res.at[0], r_ss.at[0], r_rs.at[0], right)
-    res_left = remote(res.at[1], res.at[2], r_ss.at[1], r_rs.at[1], left)
-    pl.when(has_right)(res_right.start)
-    pl.when(has_left)(res_left.start)
     arrived(slot_of(4))
 
     lane = lax.broadcasted_iota(jnp.int32, (1, WIDE), 1)
@@ -162,40 +156,44 @@
         valid = frame < limit
         key = kv[8 * part : 8 * part + 8, 0].reshape(128, WIDE)
         value = kv[8 * part : 8 * part + 8, 1].reshape(128, WIDE)
+        one = jnp.ones_like(value)
         result = []
         for half in range(2):
             scores = lax.dot_general(queries[half], key, (((1,), (1,)), ((), ())), preferred_element_type=F32)
             scores = jnp.where(valid, scores, -1e30)
             top = jnp.max(scores, axis=-1, keepdims=True)
-            powered = jnp.exp(scores - top)
-            total = jnp.sum(powered, axis=-1, keepdims=True)
-            result.append((top, total, jnp.dot(powered.astype(BF16), value, preferred_element_type=F32)))
+            powered = jnp.exp(scores - top).astype(BF16)
+            summed = jnp.where(low, value, one) if half == 0 else jnp.where(low, one, value)
+            result.append((top, jnp.dot(powered, summed, preferred_element_type=F32)))
         return result
 
     near = chunk(0)
+    res_right = remote(res.at[1], res.at[0], r_ss.at[0], r_rs.at[0], right)
+    res_left = remote(res.at[1], res.at[2], r_ss.at[1], r_rs.at[1], left)
+    pl.when(has_right)(res_right.start)
+    pl.when(has_left)(res_left.start)
     for slot in range(9, 16):
         arrived(slot)
     far = chunk(1)
 
-    home = 8 * lax.rem(lax.broadcasted_iota(jnp.int32, (512, WIDE), 0) // ROWS, 4)
-    wide_lane = lax.broadcasted_iota(jnp.int32, (512, WIDE), 1) - home
+    tops = []
+    sums = []
+    for half in range(2):
+        top_a, sum_a = near[half]
+        top_b, sum_b = far[half]
+        top = jnp.maximum(top_a, top_b)
+        tops.append(top)
+        sums.append(jnp.exp(top_a - top) * sum_a + jnp.exp(top_b - top) * sum_b)
+    total = pltpu.roll(jnp.where(low, sums[1], sums[0]), HEAD, 1)
+    a_send[:, :64] = (jnp.where(low, sums[0], sums[1]) / total).astype(BF16).reshape(SLAB, 64, WIDE)
+    level = jnp.where(low, tops[0], tops[1]) + jnp.log(total)
+    block = lax.rem(lax.broadcasted_iota(jnp.int32, (512, WIDE), 0) // ROWS, 4)
+    place_of = lax.rem(lax.broadcasted_iota(jnp.int32, (512, WIDE), 1), HEAD) - 8 * block
     stats = jnp.zeros((512, WIDE), F32)
-    tiles = []
-    for half in range(2):
-        top_a, total_a, values_a = near[half]
-        top_b, total_b, values_b = far[half]
-        top = jnp.maximum(top_a, top_b)
-        grow_a = jnp.exp(top_a - top)
-        grow_b = jnp.exp(top_b - top)
-        total = grow_a * total_a + grow_b * total_b
-        inverse = 1.0 / total
-        tiles.append((grow_a * inverse) * values_a + (grow_b * inverse) * values_b)
-        level = top + jnp.log(total)
-        for step in range(3):
-            rounded = level.astype(BF16).astype(F32)
-            stats = jnp.where(wide_lane == 3 * half + step, rounded, stats)
-            level = level - rounded
-    a_send[:, :64] = jnp.where(low, tiles[0], tiles[1]).astype(BF16).reshape(SLAB, 64, WIDE)
+    for step in range(3):
+        rounded = level.astype(BF16).astype(F32)
+        stats = jnp.where(place_of == step, rounded, stats)
+        level = level - rounded
     a_send[:, 64:] = jnp.sum(stats.reshape(SLAB, 4, ROWS, WIDE), axis=1).astype(BF16)
 
     for step in slab_steps:
@@ -204,12 +202,9 @@
     a_recv[xc] = a_send[xc]
     row_id = lax.broadcasted_iota(jnp.int32, (WIDE, WIDE), 0)
     col_id = lax.broadcasted_iota(jnp.int32, (WIDE, WIDE), 1)
-    part_id = lax.rem(row_id, 8)
+    same_half = (row_id // HEAD == col_id // HEAD) & (lax.rem(row_id, 8) < 3)
     picks = [
-        jnp.where(
-            (row_id // 8 == g) & (part_id >= 3 * (col_id // HEAD)) & (part_id < 3 * (col_id // HEAD) + 3), 1.0, 0.0
-        ).astype(BF16)
-        for g in range(4)
+        jnp.where(same_half & (lax.rem(row_id, HEAD) // 8 == g), 1.0, 0.0).astype(BF16) for g in range(4)
     ]
     for step in slab_steps[::-1]:
         sender = lax.rem(xc + SLAB - step, SLAB)

time: 35.5 us -> 35.3 us (level)
  no operation moved by 1% of the time
where the time goes in v4:
time: 35.3 us; the launch traced here: 35.1 us
  Pallas kernels  33.8 us (96%)
  between operations  0.66 us (2%)
  local copies, waits for them, and re-layouts  0.62 us (2%)
    pallas_call x1, Pallas kernels, on_device(): pl.pallas_call(kernel, out_shape=jax.ShapeDtypeStruct((ROWS, 1024), BF16)...  33.8 us

profile of v4, /device:TPU:1, one launch (start us, length us, event | category | flops | bytes accessed | tf_op | source)
XLA Modules:
  0.0 35.1 jit_solution(7397573277014711503)
XLA Ops:
  0.7 33.8 %conformer.1 = bf16[16,1024]{1,0:T(8,128)(2,1)S(1)} custom-call(bf16[16,512]{1,0:T(8,128)(2,1)} %q_hbm.1, bf16[16,512]{1,0:T(8,128)(2,1)} %k_hbm.1, bf16[16,512]{1,0:T(8,128)(2,1)} %v_hbm.1, bf16[16,1024]{1,0:T(8,128)(2,1)} %res_hbm.1, s32[1]{0:T(128)S(6)} %copy.15.len_ref, bf16[512,1024]{1,0:T(8,128)(2,1)} %wo_hbm.1, f32[1,1024]{1,0:T(1,128)} %bitcast.4, ...), custom_call_target="tpu_custom_call" | custom-call | tf_op jit(solution)/shard_map/conformer/pallas_call | solution.py:299
  34.5 0.6 %copy.16 = bf16[16,1024]{1,0:T(8,128)(2,1)} copy(bf16[16,1024]{1,0:T(8,128)(2,1)S(1)} %conformer.1) | data formatting | bytes 65536

commit v5 on v4

--- a/solution.py
+++ b/solution.py
@@ -217,7 +217,7 @@
         ctx_own[g] = (jnp.sum(weights * parts, axis=0) / jnp.sum(weights, axis=0)).astype(BF16)
 
     edges = []
-    for slab in (1, 2, 3, 0):
+    for slab in (1, 2, 0, 3):
         home_device = member(slab) * SLAB + xc
         for place in (0, 2, 1):
             target = home_device + 1 - place
@@ -233,6 +233,8 @@
             pl.when(exists)(copy.start)
             edges.append((exists, copy))
     ctx[mine, 1] = ctx_own[mine]
+    for copy in sent:
+        copy.wait_send()
 
     for load in loads[4:]:
         load.wait()
@@ -276,8 +278,6 @@
     activated = (shifted * jax.nn.sigmoid(shifted)).astype(BF16)
     out_ref[...] = (mixed[ROWS : 2 * ROWS] + jnp.dot(activated, wc[...], preferred_element_type=F32)).astype(BF16)
 
-    for copy in sent:
-        copy.wait_send()
     pl.when(has_right)(res_right.wait_send)
     pl.when(has_left)(res_left.wait_send)
     for exists, copy in edges:

time: 35.3 us -> 35.2 us (level)
  no operation moved by 1% of the time
where the time goes in v5:
time: 35.2 us; the launch traced here: 35.1 us
  Pallas kernels  33.8 us (96%)
  between operations  0.66 us (2%)
  local copies, waits for them, and re-layouts  0.62 us (2%)
    pallas_call x1, Pallas kernels, on_device(): pl.pallas_call(kernel, out_shape=jax.ShapeDtypeStruct((ROWS, 1024), BF16)...  33.8 us

profile of v5, /device:TPU:1, one launch (start us, length us, event | category | flops | bytes accessed | tf_op | source)
XLA Modules:
  0.0 35.1 jit_solution(15523792891590302302)
XLA Ops:
  0.7 33.8 %conformer.1 = bf16[16,1024]{1,0:T(8,128)(2,1)S(1)} custom-call(bf16[16,512]{1,0:T(8,128)(2,1)} %q_hbm.1, bf16[16,512]{1,0:T(8,128)(2,1)} %k_hbm.1, bf16[16,512]{1,0:T(8,128)(2,1)} %v_hbm.1, bf16[16,1024]{1,0:T(8,128)(2,1)} %res_hbm.1, s32[1]{0:T(128)S(6)} %copy.15.len_ref, bf16[512,1024]{1,0:T(8,128)(2,1)} %wo_hbm.1, f32[1,1024]{1,0:T(1,128)} %bitcast.4, ...), custom_call_target="tpu_custom_call" | custom-call | tf_op jit(solution)/shard_map/conformer/pallas_call | solution.py:299
  34.4 0.6 %copy.16 = bf16[16,1024]{1,0:T(8,128)(2,1)} copy(bf16[16,1024]{1,0:T(8,128)(2,1)S(1)} %conformer.1) | data formatting | bytes 65536

commit v6 on v5

--- a/solution.py
+++ b/solution.py
@@ -217,21 +217,23 @@
         ctx_own[g] = (jnp.sum(weights * parts, axis=0) / jnp.sum(weights, axis=0)).astype(BF16)
 
     edges = []
-    for slab in (1, 2, 0, 3):
+    mains = []
+    for turn in (2, 1, 3, 0):
+        slab = lax.rem(mine + turn, 4)
         home_device = member(slab) * SLAB + xc
-        for place in (0, 2, 1):
+        for place in (0, 2, 1) if turn else (0, 2):
             target = home_device + 1 - place
-            if place == 1:
-                exists = slab != mine
-                target = home_device
-            else:
-                exists = (target >= 0) & (target < 128)
             copy = remote(
                 ctx_own.at[slab], ctx.at[mine, place], c_ss.at[slab, place], c_rs.at[mine, place],
                 jnp.clip(target, 0, 127),
             )
-            pl.when(exists)(copy.start)
-            edges.append((exists, copy))
+            if place == 1:
+                copy.start()
+                mains.append(copy)
+            else:
+                exists = (target >= 0) & (target < 128)
+                pl.when(exists)(copy.start)
+                edges.append((exists, copy))
     ctx[mine, 1] = ctx_own[mine]
     for copy in sent:
         copy.wait_send()
@@ -280,6 +282,8 @@
 
     pl.when(has_right)(res_right.wait_send)
     pl.when(has_left)(res_left.wait_send)
+    for copy in mains:
+        copy.wait_send()
     for exists, copy in edges:
         pl.when(exists)(copy.wait_send)
 

time: 35.2 us -> 35.4 us (level)
  no operation moved by 1% of the time
where the time goes in v6:
time: 35.4 us; the launch traced here: 35.2 us
  Pallas kernels  33.9 us (96%)
  between operations  0.66 us (2%)
  local copies, waits for them, and re-layouts  0.62 us (2%)
    pallas_call x1, Pallas kernels, on_device(): pl.pallas_call(kernel, out_shape=jax.ShapeDtypeStruct((ROWS, 1024), BF16)...  33.9 us

profile of v6, /device:TPU:1, one launch (start us, length us, event | category | flops | bytes accessed | tf_op | source)
XLA Modules:
  0.0 35.2 jit_solution(1376780105746301847)
XLA Ops:
  0.7 33.9 %conformer.1 = bf16[16,1024]{1,0:T(8,128)(2,1)S(1)} custom-call(bf16[16,512]{1,0:T(8,128)(2,1)} %q_hbm.1, bf16[16,512]{1,0:T(8,128)(2,1)} %k_hbm.1, bf16[16,512]{1,0:T(8,128)(2,1)} %v_hbm.1, bf16[16,1024]{1,0:T(8,128)(2,1)} %res_hbm.1, s32[1]{0:T(128)S(6)} %copy.15.len_ref, bf16[512,1024]{1,0:T(8,128)(2,1)} %wo_hbm.1, f32[1,1024]{1,0:T(1,128)} %bitcast.4, ...), custom_call_target="tpu_custom_call" | custom-call | tf_op jit(solution)/shard_map/conformer/pallas_call | solution.py:303
  34.6 0.6 %copy.16 = bf16[16,1024]{1,0:T(8,128)(2,1)} copy(bf16[16,1024]{1,0:T(8,128)(2,1)S(1)} %conformer.1) | data formatting | bytes 65536
